TPU v7x, 32 devices: a whole 2x2x4 slice. The times are simulated.
32 devices in a mesh: parts: 2 (over x), rows: 16 (over z, y, core).
Axes of the slice: x: 2, y: 2, z: 4, core: 2. Of those that a mesh axis runs over, the one named last changes fastest.
Arguments:
- rhs: float32 [3, 12288, 256], P(None, 'rows', 'parts'), parts along dimension 2, may hold values from -6 to 6
- diag_inv: float32 [3, 12288, 768], P(None, 'rows'), may hold values from -0.21875 to 0.21875
- tiles: float32 [2, 32, 768, 768], P(None, 'rows'), may hold values from -0.15625 to 0.15625
- dest: int32 [2, 16, 2], P(None, 'rows'), may hold values from 0 to 15, all different within a row; in each aligned block of 16 rows (0 to 15, 16 to 31, ..., all dimensions but the last counted through in order) at most 4 rows name the same one
- obs_weight: float32 [12288], P('rows'), may hold values from -0.108253175 to 0.108253175, as said below
Outputs:
- solution: float32 [3, 12288, 256], P(None, 'rows', 'parts'), parts along dimension 2
- observed: float32 [256], P('parts'), parts along dimension 0
There are 2 independent parts, one for each index of `parts`. A program takes and returns all parts, laid end to end along the dimension named above; an argument that names none is the same for every part. Nothing has to cross between parts.
Inputs may be any that keep to these rules, and one draw needn't show every extreme that they name: `dest`: in each of the two levels, the two entries of a supernode differ, and no supernode of the next level is named more than 4 times. `obs_weight`: finite weights.
All inputs are finite; a program needn't handle non-finite values.
Results may differ from a plain program's by a relative error of at most 0.00029.
Values sent between devices are 32-bit elements; how exact they have to be, the bound alone decides.
No kernel may reach another device: no remote copies, remote signals or barrier semaphores. Data moves between devices by JAX's collectives and lax.ppermute only.
A program may use at most 128 MiB of HBM per device.

v0:
```python
import jax
import jax.numpy as jnp
from jax import lax
from jax.sharding import PartitionSpec as P


def collect_updates(solved_block, tiles_level, pattern_level):
    products = jnp.einsum(
        "kab,bc->kac",
        tiles_level,
        solved_block,
        precision=lax.Precision.HIGHEST,
        preferred_element_type=jnp.float32,
    )
    block_rows = solved_block.shape[0]
    width = products.shape[2]
    count = lax.axis_size("rows")
    sliced = lax.all_to_all(products, "rows", split_axis=1, concat_axis=0, tiled=True)
    owners = jnp.arange(count, dtype=jnp.int32)
    flat_targets = pattern_level.reshape(-1)
    matches = (owners[:, None] == flat_targets[None, :]).astype(jnp.float32)
    partial_value = jnp.einsum("mq,qac->mac", matches, sliced, precision=lax.Precision.HIGHEST)
    returned = lax.all_to_all(partial_value, "rows", split_axis=0, concat_axis=0, tiled=True)
    return returned.reshape(block_rows, width)


def body(rhs, diag_inv, tiles, dest, obs_weight):
    pattern = lax.all_gather(dest, "rows", axis=1, tiled=True)
    current = rhs[0]
    solved_levels = []
    solved_block = current
    for section in range(3):
        solved_block = jnp.dot(
            diag_inv[section],
            current,
            precision=lax.Precision.HIGHEST,
            preferred_element_type=jnp.float32,
        )
        solved_levels.append(solved_block)
        if section < 2:
            current = rhs[section + 1] - collect_updates(
                solved_block, tiles[section], pattern[section]
            )
    partial_sum = jnp.dot(
        obs_weight,
        solved_block,
        precision=lax.Precision.HIGHEST,
        preferred_element_type=jnp.float32,
    )
    observed = lax.psum(partial_sum, "rows")
    return (jnp.stack(solved_levels), observed)


def solution(mesh):
    in_specs = (
        P(None, "rows", "parts"),
        P(None, "rows", None),
        P(None, "rows", None, None),
        P(None, "rows", None),
        P("rows"),
    )
    out_specs = (P(None, "rows", "parts"), P("parts"))
    return jax.shard_map(body, mesh=mesh, in_specs=in_specs, out_specs=out_specs, check_vma=False)
```

profile of v0, /device:TPU:0, one launch (start us, length us, event | category | flops | bytes accessed | tf_op | source)
XLA Modules:
  0.0 156.5 jit_solution(14306570408259959369)
XLA Ops:
  0.6 3.7 %fusion.10 = f32[768,128]{1,0:T(8,128)S(1)} fusion(f32[3,768,768]{2,1,0:T(8,128)} %param.6, f32[3,768,128]{2,1,0:T(8,128)} %param.5), kind=kOutput, calls=%fused_computation.10 | convolution fusion | flops 905969664 | bytes 3145728 | tf_op jit(solution)/shard_map/dot_general | solution.py:33
  4.3 7.4 %fusion.15 = f32[2,768,128]{1,2,0:T(8,128)S(1)} fusion(f32[2,2,768,768]{3,2,1,0:T(8,128)} %param.7, f32[768,128]{1,0:T(8,128)S(1)} %fusion.10), kind=kOutput, calls=%fused_computation.15 | convolution fusion | flops 1811939328 | bytes 5898240 | tf_op jit(solution)/shard_map/kab,bc->kac/dot_general | solution.py:8
  11.7 1.2 copy.23
  12.9 7.5 %all-to-all-start = ((f32[2,768,128]{2,0,1:T(2,128)}), f32[2,768,128]{2,0,1:T(2,128)S(1)}, u32[]{:S(2)}, u32[]{:S(2)}) async-start(f32[2,768,128]{2,0,1:T(2,128)} %copy.23), calls=%async_computation | async-start | bytes 1572864 | tf_op jit(solution)/shard_map/all_to_all | solution.py:18
  20.4 29.2 %all_gather.3 = s32[2,16,2]{2,0,1:T(2,128)S(1)} all-gather(s32[2,1,2]{2,0,1:T(2,128)S(1)} %bitcast.82), channel_id=1, replica_groups=mesh['parts'=2,'rows'=16] {'rows'}, dimensions={1}, use_global_device_ids=true | all-gather | bytes 272 | tf_op jit(solution)/shard_map/all_gather | solution.py:28
  49.8 0.6 copy.25
  50.5 0.4 fusion.29
  50.8 0.1 copy.26
  51.0 16.7 %all_to_all.46 = f32[16,48,128]{2,1,0:T(8,128)S(1)} all-to-all(f32[16,48,128]{2,1,0:T(8,128)S(1)} %copy.26), channel_id=1, replica_groups=mesh['parts'=2,'rows'=16] {'rows'}, dimensions={0} | all-to-all | bytes 786432 | tf_op jit(solution)/shard_map/all_to_all | solution.py:23
  67.8 3.8 %fusion.8 = f32[128,768]{1,0:T(8,128)S(1)} fusion(f32[3,768,768]{2,1,0:T(8,128)} %param.6, f32[1,768,128]{2,1,0:T(8,128)S(1)} %bitcast_subtract_fusion.1), kind=kOutput, calls=%fused_computation.8 | convolution fusion | flops 905969664 | bytes 3145728 | tf_op jit(solution)/shard_map/dot_general | solution.py:33
  71.5 5.0 %fusion.18 = f32[2,768,128]{1,2,0:T(8,128)S(1)} fusion(f32[2,2,768,768]{3,2,1,0:T(8,128)S(1)} %copy-done, f32[128,768]{1,0:T(8,128)S(1)} %fusion.8), kind=kOutput, calls=%fused_computation.16 | convolution fusion | flops 1811939328 | bytes 5898240 | tf_op jit(solution)/shard_map/kab,bc->kac/dot_general | solution.py:8
  76.5 1.2 copy.28
  77.7 3.6 %all-to-all-start.2 = ((f32[2,768,128]{2,0,1:T(2,128)}), f32[2,768,128]{2,0,1:T(2,128)S(1)}, u32[]{:S(2)}, u32[]{:S(2)}) async-start(f32[2,768,128]{2,0,1:T(2,128)} %copy.28), calls=%async_computation.2 | async-start | bytes 1572864 | tf_op jit(solution)/shard_map/all_to_all | solution.py:18
  81.4 18.6 %all-to-all-done.2 = f32[2,768,128]{2,0,1:T(2,128)S(1)} async-done(((f32[2,768,128]{2,0,1:T(2,128)}), f32[2,768,128]{2,0,1:T(2,128)S(1)}, u32[]{:S(2)}, u32[]{:S(2)}) %all-to-all-start.2) | async-done | bytes 786464 | tf_op jit(solution)/shard_map/all_to_all | solution.py:18
  100.0 0.6 copy.30
  100.6 0.4 fusion.32
  101.0 0.9 copy.31
  101.9 5.3 %all-to-all-start.3 = ((f32[16,48,128]{2,1,0:T(8,128)}), f32[16,48,128]{2,1,0:T(8,128)S(1)}, u32[]{:S(2)}, u32[]{:S(2)}) async-start(f32[16,48,128]{2,1,0:T(8,128)} %copy.31), calls=%async_computation.3 | async-start | bytes 786432 | tf_op jit(solution)/shard_map/all_to_all | solution.py:23
  107.3 0.2 copy.27
  107.4 12.0 %all-to-all-done.3 = f32[16,48,128]{2,1,0:T(8,128)S(1)} async-done(((f32[16,48,128]{2,1,0:T(8,128)}), f32[16,48,128]{2,1,0:T(8,128)S(1)}, u32[]{:S(2)}, u32[]{:S(2)}) %all-to-all-start.3) | async-done | bytes 393248 | tf_op jit(solution)/shard_map/all_to_all | solution.py:23
  119.4 3.7 %fusion.6 = f32[128,768]{0,1:T(8,128)S(1)} fusion(f32[3,768,768]{2,1,0:T(8,128)} %param.6, f32[1,768,128]{2,1,0:T(8,128)S(1)} %bitcast_subtract_fusion), kind=kOutput, calls=%fused_computation.6 | convolution fusion | flops 905969664 | bytes 3145728 | tf_op jit(solution)/shard_map/dot_general | solution.py:33
  123.1 0.3 convolution_bitcast_fusion
  123.4 32.0 %psum.7 = f32[128]{0:T(128)} all-reduce(f32[128]{0:T(128)S(1)} %convolution_bitcast_fusion), channel_id=1, replica_groups=mesh['parts'=2,'rows'=16] {'rows'}, use_global_device_ids=true, to_apply=%region_0.0 | all-reduce | flops 128 | bytes 1024 | tf_op jit(solution)/shard_map/psum | solution.py:50
  155.4 1.1 pad_maximum_fusion
  (17 shorter events, 0.4 us)
Async XLA Ops:
  11.7 8.7 %copy-start.3 = (s32[2,1,2]{2,1,0:T(1,128)S(1)}, s32[2,1,2]{2,1,0:T(1,128)}, u32[]{:S(2)}) copy-start(s32[2,1,2]{2,1,0:T(1,128)} %param.8) | copy-start | bytes 52
  12.9 54.8 %copy-start.1 = (f32[3,768,128]{2,1,0:T(8,128)S(1)}, f32[3,768,128]{2,1,0:T(8,128)}, u32[]{:S(2)}) copy-start(f32[3,768,128]{2,1,0:T(8,128)} %param.5) | copy-start | bytes 3538948
  12.9 36.9 %all-to-all-start = ((f32[2,768,128]{2,0,1:T(2,128)}), f32[2,768,128]{2,0,1:T(2,128)S(1)}, u32[]{:S(2)}, u32[]{:S(2)}) async-start(f32[2,768,128]{2,0,1:T(2,128)} %copy.23), calls=%async_computation | async-start | bytes 1572864 | tf_op jit(solution)/shard_map/all_to_all | solution.py:18
  49.8 21.8 %copy-start = (f32[2,2,768,768]{3,2,1,0:T(8,128)S(1)}, f32[2,2,768,768]{3,2,1,0:T(8,128)}, u32[]{:S(2)}) copy-start(f32[2,2,768,768]{3,2,1,0:T(8,128)} %param.7) | copy-start | bytes 28311556
  77.7 22.3 %all-to-all-start.2 = ((f32[2,768,128]{2,0,1:T(2,128)}), f32[2,768,128]{2,0,1:T(2,128)S(1)}, u32[]{:S(2)}, u32[]{:S(2)}) async-start(f32[2,768,128]{2,0,1:T(2,128)} %copy.28), calls=%async_computation.2 | async-start | bytes 1572864 | tf_op jit(solution)/shard_map/all_to_all | solution.py:18
  100.0 7.2 %copy-start.2 = (f32[768]{0:T(1024)S(1)}, f32[768]{0:T(1024)}, u32[]{:S(2)}) copy-start(f32[768]{0:T(1024)} %param.9) | copy-start | bytes 9220
  101.9 17.5 %all-to-all-start.3 = ((f32[16,48,128]{2,1,0:T(8,128)}), f32[16,48,128]{2,1,0:T(8,128)S(1)}, u32[]{:S(2)}, u32[]{:S(2)}) async-start(f32[16,48,128]{2,1,0:T(8,128)} %copy.31), calls=%async_computation.3 | async-start | bytes 786432 | tf_op jit(solution)/shard_map/all_to_all | solution.py:23
where the time goes:
time: 157 us
  blocking collectives  77.9 us (50%)
  waiting for transfers between devices  30.5 us (19%)
  matrix products  24.5 us (16%)
  starting transfers between devices  16.5 us (11%)
  local copies, waits for them, and re-layouts  5.05 us (3%)
    psum x1, blocking collectives, body(): observed = lax.psum(partial_sum, 'rows')  32 us
    all_gather x1, blocking collectives, body(): pattern = lax.all_gather(dest, 'rows', axis=1, tiled=True)  29.2 us
    all_to_all x2, waiting for transfers between devices, collect_updates(): lax.all_to_all(products, 'rows', split_axis=1, concat_axis=0, tiled=True)  18.6 us
    all_to_all x1, blocking collectives, collect_updates(): lax.all_to_all(partial_value, 'rows', split_axis=0, concat_axis=0, tiled=...  16.7 us
    dot_general x2, matrix products, collect_updates(): jnp.einsum('kab,bc->kac', tiles_level, solved_block, precision=lax.Precis...  12.3 us
    all_to_all x1, waiting for transfers between devices, collect_updates(): lax.all_to_all(partial_value, 'rows', split_axis=0, concat_axis=0, tiled=...  12 us
    all_to_all x2, starting transfers between devices, collect_updates(): lax.all_to_all(products, 'rows', split_axis=1, concat_axis=0, tiled=True)  11.2 us
    dot_general x3, matrix products, body(): jnp.dot(diag_inv[section], current, precision=lax.Precision.HIGHEST, pref...  11.1 us
  transfers between devices with their start and end apart: 3, of which 2 were waited for; matrix products, arithmetic and copies ran while one was open for 0% of the time, Pallas kernels for 0%

commit v1 on v0

--- a/solution.py
+++ b/solution.py
@@ -47,7 +47,7 @@
         precision=lax.Precision.HIGHEST,
         preferred_element_type=jnp.float32,
     )
-    observed = lax.psum(partial_sum, "rows")
+    observed = jnp.sum(lax.all_gather(partial_sum, axis_name="rows"), 0)
     return (jnp.stack(solved_levels), observed)
 
 

time: 157 us -> 145 us (0.924)
  blocking collectives: 77.9 us -> 65 us
    psum x1 -> x0, blocking collectives: 32 us -> none  [body(): observed = lax.psum(partial_sum, 'rows')]
    all_gather x0 -> x1, blocking collectives: none -> 19.1 us  [body(): observed = jnp.sum(lax.all_gather(partial_sum, axis_name='rows'), 0)]
where the time goes in v1:
time: 145 us; the launch traced here: 144 us
  blocking collectives  65 us (45%)
  waiting for transfers between devices  30.5 us (21%)
  matrix products  24.5 us (17%)
  starting transfers between devices  16.5 us (11%)
  local copies, waits for them, and re-layouts  5.05 us (3%)
  other arithmetic  1.73 us (1%)
    all_gather x1, blocking collectives, body(): pattern = lax.all_gather(dest, 'rows', axis=1, tiled=True)  29.2 us
    all_gather x1, blocking collectives, body(): observed = jnp.sum(lax.all_gather(partial_sum, axis_name='rows'), 0)  19.1 us
    all_to_all x2, waiting for transfers between devices, collect_updates(): lax.all_to_all(products, 'rows', split_axis=1, concat_axis=0, tiled=True)  18.6 us
    all_to_all x1, blocking collectives, collect_updates(): lax.all_to_all(partial_value, 'rows', split_axis=0, concat_axis=0, tiled=...  16.7 us
    dot_general x2, matrix products, collect_updates(): jnp.einsum('kab,bc->kac', tiles_level, solved_block, precision=lax.Precis...  12.3 us
    all_to_all x1, waiting for transfers between devices, collect_updates(): lax.all_to_all(partial_value, 'rows', split_axis=0, concat_axis=0, tiled=...  12 us
    all_to_all x2, starting transfers between devices, collect_updates(): lax.all_to_all(products, 'rows', split_axis=1, concat_axis=0, tiled=True)  11.2 us
    dot_general x3, matrix products, body(): jnp.dot(diag_inv[section], current, precision=lax.Precision.HIGHEST, pref...  11.1 us
  transfers between devices with their start and end apart: 3, of which 2 were waited for; matrix products, arithmetic and copies ran while one was open for 0% of the time, Pallas kernels for 0%

profile of v1, /device:TPU:0, one launch (start us, length us, event | category | flops | bytes accessed | tf_op | source)
XLA Modules:
  0.0 144.2 jit_solution(5514744558656500553)
XLA Ops:
  0.6 3.7 %fusion.10 = f32[768,128]{1,0:T(8,128)S(1)} fusion(f32[3,768,768]{2,1,0:T(8,128)} %param.6, f32[3,768,128]{2,1,0:T(8,128)} %param.5), kind=kOutput, calls=%fused_computation.10 | convolution fusion | flops 905969664 | bytes 3145728 | tf_op jit(solution)/shard_map/dot_general | solution.py:33
  4.3 7.4 %fusion.15 = f32[2,768,128]{1,2,0:T(8,128)S(1)} fusion(f32[2,2,768,768]{3,2,1,0:T(8,128)} %param.7, f32[768,128]{1,0:T(8,128)S(1)} %fusion.10), kind=kOutput, calls=%fused_computation.15 | convolution fusion | flops 1811939328 | bytes 5898240 | tf_op jit(solution)/shard_map/kab,bc->kac/dot_general | solution.py:8
  11.7 1.2 copy.23
  12.9 7.5 %all-to-all-start = ((f32[2,768,128]{2,0,1:T(2,128)}), f32[2,768,128]{2,0,1:T(2,128)S(1)}, u32[]{:S(2)}, u32[]{:S(2)}) async-start(f32[2,768,128]{2,0,1:T(2,128)} %copy.23), calls=%async_computation | async-start | bytes 1572864 | tf_op jit(solution)/shard_map/all_to_all | solution.py:18
  20.4 29.2 %all_gather.9 = s32[2,16,2]{2,0,1:T(2,128)S(1)} all-gather(s32[2,1,2]{2,0,1:T(2,128)S(1)} %bitcast.84), channel_id=1, replica_groups=mesh['parts'=2,'rows'=16] {'rows'}, dimensions={1}, use_global_device_ids=true | all-gather | bytes 272 | tf_op jit(solution)/shard_map/all_gather | solution.py:28
  49.8 0.6 copy.25
  50.5 0.4 fusion.29
  51.0 16.7 %all_to_all.46 = f32[16,48,128]{2,1,0:T(8,128)S(1)} all-to-all(f32[16,48,128]{2,1,0:T(8,128)S(1)} %copy.26), channel_id=1, replica_groups=mesh['parts'=2,'rows'=16] {'rows'}, dimensions={0} | all-to-all | bytes 786432 | tf_op jit(solution)/shard_map/all_to_all | solution.py:23
  67.8 3.8 %fusion.8 = f32[128,768]{1,0:T(8,128)S(1)} fusion(f32[3,768,768]{2,1,0:T(8,128)} %param.6, f32[1,768,128]{2,1,0:T(8,128)S(1)} %bitcast_subtract_fusion.1), kind=kOutput, calls=%fused_computation.8 | convolution fusion | flops 905969664 | bytes 3145728 | tf_op jit(solution)/shard_map/dot_general | solution.py:33
  71.5 5.0 %fusion.18 = f32[2,768,128]{1,2,0:T(8,128)S(1)} fusion(f32[2,2,768,768]{3,2,1,0:T(8,128)S(1)} %copy-done, f32[128,768]{1,0:T(8,128)S(1)} %fusion.8), kind=kOutput, calls=%fused_computation.16 | convolution fusion | flops 1811939328 | bytes 5898240 | tf_op jit(solution)/shard_map/kab,bc->kac/dot_general | solution.py:8
  76.5 1.2 copy.28
  77.7 3.6 %all-to-all-start.2 = ((f32[2,768,128]{2,0,1:T(2,128)}), f32[2,768,128]{2,0,1:T(2,128)S(1)}, u32[]{:S(2)}, u32[]{:S(2)}) async-start(f32[2,768,128]{2,0,1:T(2,128)} %copy.28), calls=%async_computation.2 | async-start | bytes 1572864 | tf_op jit(solution)/shard_map/all_to_all | solution.py:18
  81.4 18.6 %all-to-all-done.2 = f32[2,768,128]{2,0,1:T(2,128)S(1)} async-done(((f32[2,768,128]{2,0,1:T(2,128)}), f32[2,768,128]{2,0,1:T(2,128)S(1)}, u32[]{:S(2)}, u32[]{:S(2)}) %all-to-all-start.2) | async-done | bytes 786464 | tf_op jit(solution)/shard_map/all_to_all | solution.py:18
  100.0 0.6 copy.30
  100.6 0.4 fusion.32
  101.0 0.9 copy.31
  101.9 5.3 %all-to-all-start.3 = ((f32[16,48,128]{2,1,0:T(8,128)}), f32[16,48,128]{2,1,0:T(8,128)S(1)}, u32[]{:S(2)}, u32[]{:S(2)}) async-start(f32[16,48,128]{2,1,0:T(8,128)} %copy.31), calls=%async_computation.3 | async-start | bytes 786432 | tf_op jit(solution)/shard_map/all_to_all | solution.py:23
  107.3 0.2 copy.27
  107.4 12.0 %all-to-all-done.3 = f32[16,48,128]{2,1,0:T(8,128)S(1)} async-done(((f32[16,48,128]{2,1,0:T(8,128)}), f32[16,48,128]{2,1,0:T(8,128)S(1)}, u32[]{:S(2)}, u32[]{:S(2)}) %all-to-all-start.3) | async-done | bytes 393248 | tf_op jit(solution)/shard_map/all_to_all | solution.py:23
  119.4 3.7 %fusion.6 = f32[128,768]{0,1:T(8,128)S(1)} fusion(f32[3,768,768]{2,1,0:T(8,128)} %param.6, f32[1,768,128]{2,1,0:T(8,128)S(1)} %bitcast_subtract_fusion), kind=kOutput, calls=%fused_computation.6 | convolution fusion | flops 905969664 | bytes 3145728 | tf_op jit(solution)/shard_map/dot_general | solution.py:33
  123.1 0.3 convolution_bitcast_fusion
  123.4 19.1 %all-gather.1 = f32[16,1,128]{2,1,0:T(1,128)S(1)} all-gather(f32[1,1,128]{2,1,0:T(1,128)S(1)} %convolution_bitcast_fusion), channel_id=2, replica_groups=mesh['parts'=2,'rows'=16] {'rows'}, dimensions={0}, use_global_device_ids=true | all-gather | bytes 8704 | tf_op jit(solution)/shard_map/all_gather | solution.py:50
  142.5 0.5 reduce_sum.9
  143.1 1.1 pad_maximum_fusion
  (18 shorter events, 0.6 us)
Async XLA Ops:
  11.7 8.7 %copy-start.3 = (s32[2,1,2]{2,1,0:T(1,128)S(1)}, s32[2,1,2]{2,1,0:T(1,128)}, u32[]{:S(2)}) copy-start(s32[2,1,2]{2,1,0:T(1,128)} %param.8) | copy-start | bytes 52
  12.9 54.8 %copy-start.1 = (f32[3,768,128]{2,1,0:T(8,128)S(1)}, f32[3,768,128]{2,1,0:T(8,128)}, u32[]{:S(2)}) copy-start(f32[3,768,128]{2,1,0:T(8,128)} %param.5) | copy-start | bytes 3538948
  12.9 36.9 %all-to-all-start = ((f32[2,768,128]{2,0,1:T(2,128)}), f32[2,768,128]{2,0,1:T(2,128)S(1)}, u32[]{:S(2)}, u32[]{:S(2)}) async-start(f32[2,768,128]{2,0,1:T(2,128)} %copy.23), calls=%async_computation | async-start | bytes 1572864 | tf_op jit(solution)/shard_map/all_to_all | solution.py:18
  49.8 21.8 %copy-start = (f32[2,2,768,768]{3,2,1,0:T(8,128)S(1)}, f32[2,2,768,768]{3,2,1,0:T(8,128)}, u32[]{:S(2)}) copy-start(f32[2,2,768,768]{3,2,1,0:T(8,128)} %param.7) | copy-start | bytes 28311556
  77.7 22.3 %all-to-all-start.2 = ((f32[2,768,128]{2,0,1:T(2,128)}), f32[2,768,128]{2,0,1:T(2,128)S(1)}, u32[]{:S(2)}, u32[]{:S(2)}) async-start(f32[2,768,128]{2,0,1:T(2,128)} %copy.28), calls=%async_computation.2 | async-start | bytes 1572864 | tf_op jit(solution)/shard_map/all_to_all | solution.py:18
  100.0 7.2 %copy-start.2 = (f32[768]{0:T(1024)S(1)}, f32[768]{0:T(1024)}, u32[]{:S(2)}) copy-start(f32[768]{0:T(1024)} %param.9) | copy-start | bytes 9220
  101.9 17.5 %all-to-all-start.3 = ((f32[16,48,128]{2,1,0:T(8,128)}), f32[16,48,128]{2,1,0:T(8,128)S(1)}, u32[]{:S(2)}, u32[]{:S(2)}) async-start(f32[16,48,128]{2,1,0:T(8,128)} %copy.31), calls=%async_computation.3 | async-start | bytes 786432 | tf_op jit(solution)/shard_map/all_to_all | solution.py:23
